TPU v7x, 32 devices: a whole 2x2x4 slice. The times are simulated.
32 devices in a mesh: seq: 4 (over y, core), tp: 8 (over z, x).
Axes of the slice: x: 2, y: 2, z: 4, core: 2. Of those that a mesh axis runs over, the one named last changes fastest.
Arguments:
- tokens: bfloat16 [2048, 8192], P('seq', 'tp'), may hold values from -6 to 6
- w_query: bfloat16 [8192, 6144], P(None, 'tp'), may hold values from -0.0625 to 0.0625
- w_key: bfloat16 [8192, 6144], P(None, 'tp'), may hold values from -0.0625 to 0.0625
- w_value: bfloat16 [8192, 6144], P(None, 'tp'), may hold values from -0.0625 to 0.0625
- w_out: bfloat16 [6144, 8192], P('tp'), may hold values from -0.109375 to 0.109375
- carry: float32 [48, 128, 128], P('tp'), may hold values from -40 to 40
Outputs:
- mixed: bfloat16 [2048, 8192], P('seq', 'tp')
All inputs are finite; a program needn't handle non-finite values.
Results may differ from a plain program's by a relative error of at most 0.0066.
Values may be sent and summed in bfloat16 or wider, within the bound.
No kernel may reach another device: no remote copies, remote signals or barrier semaphores. Data moves between devices by JAX's collectives and lax.ppermute only.
A program may use at most 192 MiB of HBM per device.

v0:
```python
import jax
import jax.numpy as jnp
from jax import lax
from jax.sharding import PartitionSpec as P

EPSILON = 1e-05


def entering(array, axis, combine, identity):
    count, place = (lax.axis_size(axis), lax.axis_index(axis))
    everything = lax.all_gather(array, axis)
    start = jnp.broadcast_to(jnp.asarray(identity, array.dtype), array.shape)

    def turn(k, before):
        reached = k < place
        new = combine(before, everything[k])
        return jnp.where(reached, new, before)

    return lax.fori_loop(0, count, turn, start)


def combine_states(earlier, latter_part):
    return earlier + latter_part


def local(tokens, w_query, w_key, w_value, w_out, carry):
    row_count = tokens.shape[0]
    head_count = carry.shape[0]
    head_size = carry.shape[1]
    proj_width = w_query.shape[1]
    segment = lax.all_gather(tokens, "tp", axis=1, tiled=True)
    query_sum = jnp.dot(segment, w_query, preferred_element_type=jnp.float32)
    key_sum = jnp.dot(segment, w_key, preferred_element_type=jnp.float32)
    value_sum = jnp.dot(segment, w_value, preferred_element_type=jnp.float32)
    query = query_sum.astype(jnp.bfloat16).reshape(row_count, head_count, head_size)
    keys_local = key_sum.astype(jnp.bfloat16).reshape(row_count, head_count, head_size)
    values_local = value_sum.astype(jnp.bfloat16).reshape(row_count, head_count, head_size)
    local_state = jnp.einsum(
        "thd,the->hde", keys_local, values_local, preferred_element_type=jnp.float32
    )
    earlier_sum = entering(local_state, "seq", combine_states, jnp.zeros_like(local_state))
    prior = carry + earlier_sum
    across = jnp.einsum(
        "thd,hde->the", query.astype(jnp.float32), prior, precision=lax.Precision.HIGHEST
    )
    causal = lax.broadcasted_iota(jnp.int32, (row_count, row_count), 0) >= lax.broadcasted_iota(
        jnp.int32, (row_count, row_count), 1
    )
    scores = jnp.einsum("thd,shd->hts", query, keys_local, preferred_element_type=jnp.float32)
    scores = jnp.where(causal[None], scores, 0.0).astype(jnp.bfloat16)
    within = jnp.einsum("hts,she->the", scores, values_local, preferred_element_type=jnp.float32)
    total = across + within
    normed = total * lax.rsqrt(jnp.mean(total * total, axis=-1, keepdims=True) + EPSILON)
    attended = normed.astype(jnp.bfloat16).reshape(row_count, proj_width)
    summed = lax.psum_scatter(
        lax.dot_general(
            w_out, attended, (((0,), (1,)), ((), ())), preferred_element_type=jnp.float32
        ),
        "tp",
        scatter_dimension=0,
        tiled=True,
    )
    return summed.T.astype(jnp.bfloat16)


def solution(mesh):
    placed = (
        P("seq", "tp"),
        P(None, "tp"),
        P(None, "tp"),
        P(None, "tp"),
        P("tp", None),
        P("tp", None, None),
    )
    return jax.shard_map(
        local, mesh=mesh, in_specs=placed, out_specs=P("seq", "tp"), check_vma=False
    )
```

profile of v0, /device:TPU:0, one launch (start us, length us, event | category | flops | bytes accessed | tf_op | source)
XLA Modules:
  0.0 496.5 jit_solution(3666014107982523729)
XLA Ops:
  6.5 0.7 all-gather.4.cloned.1.call-update
  7.3 0.0 all-gather.6.cloned.1.call-start
  7.3 129.9 %all-gather.4.cloned.1.call-done = bf16[512,8192]{1,0:T(8,128)(2,1)} async-done(((bf16[512,1024]{1,0:T(8,128)(2,1)}), bf16[512,8192]{1,0:T(8,128)(2,1)}) %all-gather.4.cloned.1.call-update) | async-done | bytes 8388624 | tf_op jit(solution)/shard_map/all_gather | solution.py:31
  137.2 12.7 %convolution_convert_fusion.2 = bf16[512,768]{1,0:T(8,128)(2,1)S(1)} fusion(bf16[512,8192]{1,0:T(8,128)(2,1)} %all-gather.4.cloned.1.call-done, bf16[8192,768]{1,0:T(8,128)(2,1)} %param.10), kind=kOutput, calls=%fused_computation.14 | convolution fusion | flops 6442844160 | bytes 21757952 | tf_op jit(solution)/shard_map/dot_general | solution.py:33
  149.9 0.3 copy.18
  150.2 12.7 %convolution_convert_fusion.1 = bf16[512,768]{1,0:T(8,128)(2,1)S(1)} fusion(bf16[512,8192]{1,0:T(8,128)(2,1)} %all-gather.4.cloned.1.call-done, bf16[8192,768]{1,0:T(8,128)(2,1)} %param.11), kind=kOutput, calls=%fused_computation.13 | convolution fusion | flops 6442844160 | bytes 21757952 | tf_op jit(solution)/shard_map/dot_general | solution.py:34
  162.9 0.3 copy.19
  163.2 1.1 fusion.9
  164.3 0.0 all-gather.6.cloned.1.call-update
  164.3 0.2 reduce-scatter.2.cloned.1.call-start
  164.6 0.8 iota_compare_fusion
  165.3 13.2 %convolution_convert_fusion = bf16[512,768]{1,0:T(8,128)(2,1)S(1)} fusion(bf16[512,8192]{1,0:T(8,128)(2,1)} %all-gather.4.cloned.1.call-done, bf16[8192,768]{1,0:T(8,128)(2,1)} %param.9), kind=kOutput, calls=%fused_computation.12 | convolution fusion | flops 6442844160 | bytes 21757952 | tf_op jit(solution)/shard_map/dot_general | solution.py:32
  178.6 0.3 copy.21
  178.9 4.2 fusion
  183.1 4.6 while.14
  183.1 1.1 add_select_fusion.2
  184.2 1.1 add_select_fusion.2
  185.4 1.1 add_select_fusion.2
  186.5 1.1 add_select_fusion.2
  187.7 2.4 fusion.5
  190.1 0.2 fusion.6
  190.3 14.8 %convolution_bitcast_fusion = f32[8192,512]{0,1:T(8,128)} fusion(bf16[512,768]{0,1:T(8,128)(2,1)S(1)} %bitcast.34, bf16[768,8192]{1,0:T(8,128)(2,1)} %param.12), kind=kOutput, calls=%fused_computation.1 | convolution fusion | flops 6442450944 | bytes 30146560 | tf_op jit(solution)/shard_map/dot_general | solution.py:56
  205.1 282.1 %reduce-scatter.2.cloned.1.call-done = f32[1024,512]{0,1:T(8,128)} async-done(((f32[8192,512]{0,1:T(8,128)}), f32[1024,512]{0,1:T(8,128)}) %reduce-scatter.2.cloned.1.call-update) | async-done | bytes 2097168 | tf_op jit(solution)/shard_map/reduce_scatter | solution.py:55
  487.2 2.7 convert_bitcast_fusion
  (7 shorter events, 0.0 us)
Async XLA Ops:
  6.5 130.7 %all-gather.4.cloned.1.call-start = ((), (), s32[]{:S(2)}) async-start(), calls=%async_computation.1 | async-start | bytes 9437184 | tf_op jit(solution)/shard_map/all_gather | solution.py:31
  7.3 175.8 %all-gather.6.cloned.1.call-start = ((), (), s32[]{:S(2)}) async-start(), calls=%async_computation.3 | async-start | bytes 1966080 | tf_op jit(solution)/shard_map/all_gather | solution.py:11
  164.3 322.9 %reduce-scatter.2.cloned.1.call-start = ((), (), s32[]{:S(2)}) async-start(), calls=%async_computation.2 | async-start | bytes 18874368 | tf_op jit(solution)/shard_map/reduce_scatter | solution.py:55
  178.9 8.8 %copy-start = (f32[6,128,128]{2,1,0:T(8,128)S(1)}, f32[6,128,128]{2,1,0:T(8,128)}, u32[]{:S(2)}) copy-start(f32[6,128,128]{2,1,0:T(8,128)} %param.13) | copy-start | bytes 1179652
Sparse Core Ops, SparseCore 0:
  9.5 127.5 all-gather.3
  164.4 17.8 all-gather.5
  205.2 281.9 reduce-scatter.1
where the time goes:
time: 497 us; the launch traced here: 496 us
  waiting for transfers between devices  413 us (83%)
  matrix products  61.1 us (12%)
  between operations  13.2 us (3%)
  other arithmetic  8.24 us (2%)
    reduce_scatter x1, waiting for transfers between devices, local(): lax.psum_scatter(lax.dot_general(w_out, attended, (((0,), (1,)), ((), ())...  282 us
    all_gather x1, waiting for transfers between devices, local(): segment = lax.all_gather(tokens, 'tp', axis=1, tiled=True)  130 us
    dot_general x1, matrix products, local(): lax.dot_general(w_out, attended, (((0,), (1,)), ((), ())), preferred_elem...  14.8 us
    dot_general x1, matrix products, local(): query_sum = jnp.dot(segment, w_query, preferred_element_type=jnp.float32)  13.2 us
    dot_general x1, matrix products, local(): key_sum = jnp.dot(segment, w_key, preferred_element_type=jnp.float32)  12.7 us
    dot_general x1, matrix products, local(): value_sum = jnp.dot(segment, w_value, preferred_element_type=jnp.float32)  12.7 us
  transfers between devices with their start and end apart: 3, of which 2 were waited for; matrix products, arithmetic and copies ran while one was open for 4% of the time, Pallas kernels for 0%

commit v1 on v0

--- a/solution.py
+++ b/solution.py
@@ -28,7 +28,12 @@
     head_count = carry.shape[0]
     head_size = carry.shape[1]
     proj_width = w_query.shape[1]
-    segment = lax.all_gather(tokens, "tp", axis=1, tiled=True)
+    ring = [tokens]
+    for hop in range(7):
+        ring.append(lax.ppermute(ring[-1], "tp", [(dev, (dev + 1) % 8) for dev in range(8)]))
+    segment = jnp.roll(
+        jnp.concatenate(ring[::-1], axis=1), (lax.axis_index("tp") + 1) * ring[0].shape[1], axis=1
+    )
     query_sum = jnp.dot(segment, w_query, preferred_element_type=jnp.float32)
     key_sum = jnp.dot(segment, w_key, preferred_element_type=jnp.float32)
     value_sum = jnp.dot(segment, w_value, preferred_element_type=jnp.float32)

time: 497 us -> 560 us (1.13)
  waiting for transfers between devices: 413 us -> 456 us
  local copies, waits for them, and re-layouts: 0.84 us -> 20.7 us
    ppermute x0 -> x7, waiting for transfers between devices: none -> 175 us  [local(): lax.ppermute(ring[-1], 'tp', [(dev, (dev + 1) % 8) for dev in range(8)])]
    all_gather x1 -> x0, waiting for transfers between devices: 130 us -> none  [local(): segment = lax.all_gather(tokens, 'tp', axis=1, tiled=True)]
    unnamed x2 -> x31, local copies, waits for them, and re-layouts: 0.01 us -> 19.8 us
  transfers between devices with their start and end apart: 3 -> 9, of which waited for: 2 -> 8; matrix products, arithmetic and copies ran while one was open for 4% -> 3% of each run, Pallas kernels for 0% -> 0%
where the time goes in v1:
time: 560 us
  waiting for transfers between devices  456 us (81%)
  matrix products  58.2 us (10%)
  local copies, waits for them, and re-layouts  20.7 us (4%)
  between operations  13.7 us (2%)
  other arithmetic  8.25 us (1%)
    reduce_scatter x1, waiting for transfers between devices, local(): lax.psum_scatter(lax.dot_general(w_out, attended, (((0,), (1,)), ((), ())...  280 us
    ppermute x7, waiting for transfers between devices, local(): lax.ppermute(ring[-1], 'tp', [(dev, (dev + 1) % 8) for dev in range(8)])  175 us
    unnamed x31, local copies, waits for them, and re-layouts  19.8 us
    dot_general x1, matrix products, local(): lax.dot_general(w_out, attended, (((0,), (1,)), ((), ())), preferred_elem...  14.8 us
    dot_general x1, matrix products, local(): query_sum = jnp.dot(segment, w_query, preferred_element_type=jnp.float32)  13.3 us
    dot_general x1, matrix products, local(): value_sum = jnp.dot(segment, w_value, preferred_element_type=jnp.float32)  12.7 us
  transfers between devices with their start and end apart: 9, of which 8 were waited for; matrix products, arithmetic and copies ran while one was open for 3% of the time, Pallas kernels for 0%

profile of v1, /device:TPU:0, one launch (start us, length us, event | category | flops | bytes accessed | tf_op | source)
XLA Modules:
  0.0 559.8 jit_solution(17653001376896906398)
XLA Ops:
  6.5 2.9 collective-permute-start
  9.5 26.5 %collective-permute-done = bf16[512,1024]{1,0:T(8,128)(2,1)S(1)} collective-permute-done((bf16[512,1024]{1,0:T(8,128)(2,1)}, bf16[512,1024]{1,0:T(8,128)(2,1)S(1)}, u32[]{:S(2)}, u32[]{:S(2)}) %collective-permute-start) | collective-permute-done | bytes 1048608 | tf_op jit(solution)/shard_map/ppermute | solution.py:33
  36.0 27.0 %collective-permute-done.1 = bf16[512,1024]{1,0:T(8,128)(2,1)S(1)} collective-permute-done((bf16[512,1024]{1,0:T(8,128)(2,1)S(1)}, bf16[512,1024]{1,0:T(8,128)(2,1)S(1)}, u32[]{:S(2)}, u32[]{:S(2)}) %collective-permute-start.1) | collective-permute-done | bytes 1048608 | tf_op jit(solution)/shard_map/ppermute | solution.py:33
  63.0 26.1 %collective-permute-done.2 = bf16[512,1024]{1,0:T(8,128)(2,1)S(1)} collective-permute-done((bf16[512,1024]{1,0:T(8,128)(2,1)S(1)}, bf16[512,1024]{1,0:T(8,128)(2,1)S(1)}, u32[]{:S(2)}, u32[]{:S(2)}) %collective-permute-start.2) | collective-permute-done | bytes 1048608 | tf_op jit(solution)/shard_map/ppermute | solution.py:33
  90.1 25.2 %collective-permute-done.3 = bf16[512,1024]{1,0:T(8,128)(2,1)S(1)} collective-permute-done((bf16[512,1024]{1,0:T(8,128)(2,1)S(1)}, bf16[512,1024]{1,0:T(8,128)(2,1)S(1)}, u32[]{:S(2)}, u32[]{:S(2)}) %collective-permute-start.3) | collective-permute-done | bytes 1048608 | tf_op jit(solution)/shard_map/ppermute | solution.py:33
  116.3 24.3 %collective-permute-done.4 = bf16[512,1024]{1,0:T(8,128)(2,1)S(1)} collective-permute-done((bf16[512,1024]{1,0:T(8,128)(2,1)S(1)}, bf16[512,1024]{1,0:T(8,128)(2,1)S(1)}, u32[]{:S(2)}, u32[]{:S(2)}) %collective-permute-start.4) | collective-permute-done | bytes 1048608 | tf_op jit(solution)/shard_map/ppermute | solution.py:33
  141.6 23.5 %collective-permute-done.5 = bf16[512,1024]{1,0:T(8,128)(2,1)} collective-permute-done((bf16[512,1024]{1,0:T(8,128)(2,1)S(1)}, bf16[512,1024]{1,0:T(8,128)(2,1)}, u32[]{:S(2)}, u32[]{:S(2)}) %collective-permute-start.5) | collective-permute-done | bytes 1048608 | tf_op jit(solution)/shard_map/ppermute | solution.py:33
  165.0 22.7 %collective-permute-done.6 = bf16[512,1024]{1,0:T(8,128)(2,1)} collective-permute-done((bf16[512,1024]{1,0:T(8,128)(2,1)}, bf16[512,1024]{1,0:T(8,128)(2,1)}, u32[]{:S(2)}, u32[]{:S(2)}) %collective-permute-start.6) | collective-permute-done | bytes 1048608 | tf_op jit(solution)/shard_map/ppermute | solution.py:33
  189.1 1.3 constant_dynamic-update-slice_fusion.14
  190.4 1.3 constant_dynamic-update-slice_fusion.13
  191.7 1.3 constant_dynamic-update-slice_fusion.12
  193.0 1.3 constant_dynamic-update-slice_fusion.11
  194.6 1.3 constant_dynamic-update-slice_fusion.8
  195.9 1.3 constant_dynamic-update-slice_fusion.7
  199.1 5.7 %copy-done.7 = bf16[512,16384]{1,0:T(8,128)(2,1)} copy-done((bf16[512,16384]{1,0:T(8,128)(2,1)}, bf16[512,16384]{1,0:T(8,128)(2,1)S(1)}, u32[]{:S(2)}) %copy-start.7) | copy-done | bytes 16777240
  204.9 9.7 %fusion.13 = bf16[512,768]{1,0:T(8,128)(2,1)S(1)} fusion(bf16[8192,768]{1,0:T(8,128)(2,1)} %param.10, bf16[512,16384]{1,0:T(8,128)(2,1)S(1)} %constant_dynamic-update-slice_fusion, s32[]{:T(128)S(6)} %select_n.39), kind=kOutput, calls=%fused_computation.18 | convolution fusion | flops 6442844160 | bytes 21757956 | tf_op jit(solution)/shard_map/dot_general | solution.py:38
  214.9 12.7 %fusion.16 = bf16[512,768]{1,0:T(8,128)(2,1)S(1)} fusion(bf16[8192,768]{1,0:T(8,128)(2,1)} %param.11, bf16[512,16384]{1,0:T(8,128)(2,1)} %copy-done.7, s32[]{:T(128)S(6)} %select_n.39), kind=kOutput, calls=%fused_computation.19 | convolution fusion | flops 6442844160 | bytes 21757956 | tf_op jit(solution)/shard_map/dot_general | solution.py:39
  230.0 13.3 %fusion.19 = bf16[512,768]{1,0:T(8,128)(2,1)S(1)} fusion(bf16[8192,768]{1,0:T(8,128)(2,1)} %param.9, bf16[512,16384]{1,0:T(8,128)(2,1)} %copy-done.7, s32[]{:T(128)S(6)} %select_n.39), kind=kOutput, calls=%fused_computation.20 | convolution fusion | flops 6442844160 | bytes 21757956 | tf_op jit(solution)/shard_map/dot_general | solution.py:37
  243.6 4.1 fusion.6
  247.7 4.6 while.14
  252.3 2.5 fusion.11
  255.1 14.8 %convolution_bitcast_fusion = f32[8192,512]{0,1:T(8,128)} fusion(bf16[512,768]{0,1:T(8,128)(2,1)S(1)} %bitcast.31, bf16[768,8192]{1,0:T(8,128)(2,1)} %param.12), kind=kOutput, calls=%fused_computation.1 | convolution fusion | flops 6442450944 | bytes 30146560 | tf_op jit(solution)/shard_map/dot_general | solution.py:61
  269.9 280.3 %reduce-scatter.2.cloned.1.call-done = f32[1024,512]{0,1:T(8,128)} async-done(((f32[8192,512]{0,1:T(8,128)}), f32[1024,512]{0,1:T(8,128)}) %reduce-scatter.2.cloned.1.call-update) | async-done | bytes 2097168 | tf_op jit(solution)/shard_map/reduce_scatter | solution.py:60
  550.2 2.7 convert_bitcast_fusion
  (48 shorter events, 14.0 us)
Async XLA Ops:
  6.5 192.5 %copy-start = (bf16[512,1024]{1,0:T(8,128)(2,1)S(1)}, bf16[512,1024]{1,0:T(8,128)(2,1)}, u32[]{:S(2)}) copy-start(bf16[512,1024]{1,0:T(8,128)(2,1)} %param.8) | copy-start | bytes 3145732
  6.5 241.2 %all-gather.3.cloned.1.call-start = ((), (), s32[]{:S(2)}) async-start(), calls=%async_computation.2 | async-start | bytes 1966080 | tf_op jit(solution)/shard_map/all_gather | solution.py:11
  6.5 29.4 %collective-permute-start = (bf16[512,1024]{1,0:T(8,128)(2,1)}, bf16[512,1024]{1,0:T(8,128)(2,1)S(1)}, u32[]{:S(2)}, u32[]{:S(2)}) collective-permute-start(bf16[512,1024]{1,0:T(8,128)(2,1)} %param.8), channel_id=1, source_target_pairs={{0,1},{1,2},{2,3},{3,4},{4,5},{5,6},{6,7},{7,0},{8,9},{9,10},{10,1... | collective-permute-start | bytes 3145736 | tf_op jit(solution)/shard_map/ppermute | solution.py:33
  36.0 27.0 %collective-permute-start.1 = (bf16[512,1024]{1,0:T(8,128)(2,1)S(1)}, bf16[512,1024]{1,0:T(8,128)(2,1)S(1)}, u32[]{:S(2)}, u32[]{:S(2)}) collective-permute-start(bf16[512,1024]{1,0:T(8,128)(2,1)S(1)} %collective-permute-done), channel_id=1, source_target_pairs={{0,1},{1,2},{2,3},{3,4},{4,5},{5,6},{6,7},{7,0},{8,9},{9,10},{10,1... | collective-permute-start | bytes 3145736 | tf_op jit(solution)/shard_map/ppermute | solution.py:33
  63.0 26.1 %collective-permute-start.2 = (bf16[512,1024]{1,0:T(8,128)(2,1)S(1)}, bf16[512,1024]{1,0:T(8,128)(2,1)S(1)}, u32[]{:S(2)}, u32[]{:S(2)}) collective-permute-start(bf16[512,1024]{1,0:T(8,128)(2,1)S(1)} %collective-permute-done.1), channel_id=1, source_target_pairs={{0,1},{1,2},{2,3},{3,4},{4,5},{5,6},{6,7},{7,0},{8,9},{9,10},{10,1... | collective-permute-start | bytes 3145736 | tf_op jit(solution)/shard_map/ppermute | solution.py:33
  89.1 1.0 copy-start.1
  90.1 25.2 %collective-permute-start.3 = (bf16[512,1024]{1,0:T(8,128)(2,1)S(1)}, bf16[512,1024]{1,0:T(8,128)(2,1)S(1)}, u32[]{:S(2)}, u32[]{:S(2)}) collective-permute-start(bf16[512,1024]{1,0:T(8,128)(2,1)S(1)} %collective-permute-done.2), channel_id=1, source_target_pairs={{0,1},{1,2},{2,3},{3,4},{4,5},{5,6},{6,7},{7,0},{8,9},{9,10},{10,1... | collective-permute-start | bytes 3145736 | tf_op jit(solution)/shard_map/ppermute | solution.py:33
  115.3 1.0 copy-start.3
  116.3 24.3 %collective-permute-start.4 = (bf16[512,1024]{1,0:T(8,128)(2,1)S(1)}, bf16[512,1024]{1,0:T(8,128)(2,1)S(1)}, u32[]{:S(2)}, u32[]{:S(2)}) collective-permute-start(bf16[512,1024]{1,0:T(8,128)(2,1)S(1)} %collective-permute-done.3), channel_id=1, source_target_pairs={{0,1},{1,2},{2,3},{3,4},{4,5},{5,6},{6,7},{7,0},{8,9},{9,10},{10,1... | collective-permute-start | bytes 3145736 | tf_op jit(solution)/shard_map/ppermute | solution.py:33
  140.6 1.0 copy-start.5
  141.6 23.5 %collective-permute-start.5 = (bf16[512,1024]{1,0:T(8,128)(2,1)S(1)}, bf16[512,1024]{1,0:T(8,128)(2,1)}, u32[]{:S(2)}, u32[]{:S(2)}) collective-permute-start(bf16[512,1024]{1,0:T(8,128)(2,1)S(1)} %collective-permute-done.4), channel_id=1, source_target_pairs={{0,1},{1,2},{2,3},{3,4},{4,5},{5,6},{6,7},{7,0},{8,9},{9,10},{10,1... | collective-permute-start | bytes 3145736 | tf_op jit(solution)/shard_map/ppermute | solution.py:33
  165.0 22.8 %collective-permute-start.6 = (bf16[512,1024]{1,0:T(8,128)(2,1)}, bf16[512,1024]{1,0:T(8,128)(2,1)}, u32[]{:S(2)}, u32[]{:S(2)}) collective-permute-start(bf16[512,1024]{1,0:T(8,128)(2,1)} %collective-permute-done.5), channel_id=1, source_target_pairs={{0,1},{1,2},{2,3},{3,4},{4,5},{5,6},{6,7},{7,0},{8,9},{9,10},{10,1... | collective-permute-start | bytes 3145736 | tf_op jit(solution)/shard_map/ppermute | solution.py:33
  165.0 33.5 %copy-start.6 = (bf16[512,1024]{1,0:T(8,128)(2,1)S(1)}, bf16[512,1024]{1,0:T(8,128)(2,1)}, u32[]{:S(2)}) copy-start(bf16[512,1024]{1,0:T(8,128)(2,1)} %copy-done.5) | copy-start | bytes 3145732
  165.0 33.6 %copy-start.4 = (bf16[512,1024]{1,0:T(8,128)(2,1)S(1)}, bf16[512,1024]{1,0:T(8,128)(2,1)}, u32[]{:S(2)}) copy-start(bf16[512,1024]{1,0:T(8,128)(2,1)} %copy-done.3) | copy-start | bytes 3145732
  165.0 33.7 %copy-start.2 = (bf16[512,1024]{1,0:T(8,128)(2,1)S(1)}, bf16[512,1024]{1,0:T(8,128)(2,1)}, u32[]{:S(2)}) copy-start(bf16[512,1024]{1,0:T(8,128)(2,1)} %copy-done.1) | copy-start | bytes 3145732
  199.1 5.8 %copy-start.7 = (bf16[512,16384]{1,0:T(8,128)(2,1)}, bf16[512,16384]{1,0:T(8,128)(2,1)S(1)}, u32[]{:S(2)}) copy-start(bf16[512,16384]{1,0:T(8,128)(2,1)S(1)} %constant_dynamic-update-slice_fusion) | copy-start | bytes 50331652
  229.0 321.2 %reduce-scatter.2.cloned.1.call-start = ((), (), s32[]{:S(2)}) async-start(), calls=%async_computation.1 | async-start | bytes 18874368 | tf_op jit(solution)/shard_map/reduce_scatter | solution.py:60
Sparse Core Ops, SparseCore 0:
  229.1 16.0 all-gather.2
  270.0 280.1 reduce-scatter.1
